TPU v7x, 32 devices: a whole 2x2x4 slice. The times are simulated.
32 devices in a mesh: req: 32 (over z, y, x, core).
Axes of the slice: x: 2, y: 2, z: 4, core: 2. Of those that a mesh axis runs over, the one named last changes fastest.
Arguments:
- hidden_in: bfloat16 [16384, 2048], P('req'), may hold values from -6 to 6
- qkv: bfloat16 [16384, 6144], P('req'), may hold values from -400 to 400
- cache: bfloat16 [128, 128, 4096], P('req'), may hold values from -400 to 400
- lengths: int32 [128], P('req'), may hold values from 2 to 128, as said below
- prefill_flag: int32 [32], P('req'), may hold values 0 or 1
- cache_slot: int32 [128], P('req'), may hold values from 0 to 127, as said below
- slot_owner: int32 [128], P('req'), may hold values from 0 to 127, as said below
- out_weight: bfloat16 [2048, 2048], replicated, may hold values from -0.125 to 0.125
Outputs:
- layer_out: bfloat16 [16384, 2048], P('req')
Inputs may be any that keep to these rules, and one draw needn't show every extreme that they name: Each slot stores exactly one request's cache; of each device's 4 requests, at least half have their cache in a slot of their own device, drawn which; slot_owner[cache_slot[r]] = r. `slot_owner`: the inverse of cache_slot. `lengths`: some slot holds exactly 128 valid positions.
All inputs are finite; a program needn't handle non-finite values. No bound on the sum of `prefill_flag` on one device may be relied on, other than what follows from the above.
Results may differ from a plain program's by a relative error of at most 0.0034.
Values may be sent and summed in bfloat16 or wider, within the bound.
A program may use at most 128 MiB of HBM per device.

v0:
```python
import math
import jax
import jax.numpy as jnp
from jax import lax
from jax.sharding import PartitionSpec as P

D = 2048
H = 16
HD = 128
TOK_DEV = 512
RD = 4
LMAX = 128


def prefill_attention(block):
    score_scale = 1.0 / math.sqrt(HD)
    queries = block[:, :D].reshape(TOK_DEV, H, HD)
    keys_new = block[:, D : 2 * D].reshape(TOK_DEV, H, HD)
    values_new = block[:, 2 * D :].reshape(TOK_DEV, H, HD)
    scores = (
        jnp.einsum("qhd,khd->hqk", queries, keys_new, preferred_element_type=jnp.float32)
        * score_scale
    )
    causal = jnp.arange(TOK_DEV)[:, None] >= jnp.arange(TOK_DEV)[None, :]
    scores = jnp.where(causal[None], scores, -jnp.inf)
    top_score = jnp.max(scores, axis=-1, keepdims=True)
    expon = jnp.exp(scores - top_score)
    totals = jnp.sum(expon, axis=-1)
    summed = jnp.einsum(
        "hqk,khd->qhd", expon.astype(jnp.bfloat16), values_new, preferred_element_type=jnp.float32
    )
    result = summed / jnp.transpose(totals)[:, :, None]
    return result.reshape(TOK_DEV, D).astype(jnp.bfloat16)


def holder_partial(queries, cache, lengths):
    score_scale = 1.0 / math.sqrt(HD)
    query_heads = queries.reshape(RD, H, HD)
    cache_keys = cache[:, :, :D].reshape(RD, LMAX, H, HD)
    cache_values = cache[:, :, D:].reshape(RD, LMAX, H, HD)
    scores = (
        jnp.einsum("rhd,rlhd->rhl", query_heads, cache_keys, preferred_element_type=jnp.float32)
        * score_scale
    )
    valid = jnp.arange(LMAX, dtype=jnp.int32)[None, None, :] < lengths[:, None, None]
    scores = jnp.where(valid, scores, -jnp.inf)
    cache_max = jnp.max(scores, axis=-1)
    expon = jnp.exp(scores - cache_max[..., None])
    cache_total = jnp.sum(expon, axis=-1)
    cache_out = jnp.einsum(
        "rhl,rlhd->rhd",
        expon.astype(jnp.bfloat16),
        cache_values,
        preferred_element_type=jnp.float32,
    )
    return (cache_out.reshape(RD, D), cache_max, cache_total)


def combine_own(request_rows, cache_out, cache_max, cache_total):
    score_scale = 1.0 / math.sqrt(HD)
    query_heads = request_rows[:, :D].reshape(RD, H, HD).astype(jnp.float32)
    keys_new = request_rows[:, D : 2 * D].reshape(RD, H, HD).astype(jnp.float32)
    values_new = request_rows[:, 2 * D :].reshape(RD, H, HD).astype(jnp.float32)
    own_score = jnp.sum(query_heads * keys_new, axis=-1) * score_scale
    joint_max = jnp.maximum(cache_max, own_score)
    cache_factor = jnp.exp(cache_max - joint_max)
    own_factor = jnp.exp(own_score - joint_max)
    numer = (
        cache_out.reshape(RD, H, HD) * cache_factor[..., None] + own_factor[..., None] * values_new
    )
    denom = cache_total * cache_factor + own_factor
    return (numer / denom[..., None]).reshape(RD, D).astype(jnp.bfloat16)


def local(hidden_in, qkv, cache, lengths, prefill_flag, cache_slot, slot_owner, out_weight):
    request_rows = qkv[:RD]
    every_query = lax.all_gather(request_rows[:, :D], "req", axis=0, tiled=True)
    held_queries = every_query[slot_owner]
    part_out, part_max, part_total = holder_partial(held_queries, cache, lengths)
    every_out, every_max, every_total = (
        lax.all_gather(part_out.astype(jnp.bfloat16), "req", axis=0, tiled=True).astype(
            part_out.dtype
        ),
        lax.all_gather(part_max.astype(jnp.bfloat16), "req", axis=0, tiled=True).astype(
            part_max.dtype
        ),
        lax.all_gather(part_total.astype(jnp.bfloat16), "req", axis=0, tiled=True).astype(
            part_total.dtype
        ),
    )
    decode_att = combine_own(
        request_rows, every_out[cache_slot], every_max[cache_slot], every_total[cache_slot]
    )
    is_prefill = prefill_flag[0] == 1

    def prefill_path(block):
        attended = prefill_attention(block)
        return jnp.dot(attended, out_weight, preferred_element_type=jnp.float32).astype(
            jnp.bfloat16
        )

    def decode_path(block):
        live = jnp.dot(decode_att, out_weight, preferred_element_type=jnp.float32).astype(
            jnp.bfloat16
        )
        return jnp.concatenate([live, jnp.zeros((TOK_DEV - RD, D), jnp.bfloat16)], axis=0)

    projected = lax.cond(is_prefill, prefill_path, decode_path, qkv)
    summed = hidden_in.astype(jnp.float32) + projected.astype(jnp.float32)
    return summed.astype(jnp.bfloat16)


def solution(mesh):
    placed = (
        P("req", None),
        P("req", None),
        P("req", None, None),
        P("req"),
        P("req"),
        P("req"),
        P("req"),
        P(),
    )
    return jax.shard_map(
        local, mesh=mesh, in_specs=placed, out_specs=P("req", None), check_vma=False
    )
```

profile of v0, /device:TPU:0, one launch (start us, length us, event | category | flops | bytes accessed | tf_op | source)
XLA Modules:
  0.0 231.2 jit_solution(15579366147625669525)
XLA Ops:
  0.7 0.7 iota_compare_fusion.1
  1.4 0.7 compare_select_fusion
  2.0 0.7 compare_select_fusion.1
  2.7 0.8 slice_bitcast_fusion.1
  3.5 0.8 multiply_bitcast_fusion
  4.3 0.1 bitcast_reduce_fusion
  4.4 44.6 %all-gather = bf16[32,4,2048]{2,1,0:T(4,128)(2,1)S(1)} all-gather(bf16[1,4,2048]{2,1,0:T(4,128)(2,1)S(1)} %slice_bitcast_fusion.1), channel_id=1, replica_groups=mesh['req'=32] {'req'}, dimensions={0}, use_global_device_ids=true | all-gather | bytes 540672 | tf_op jit(solution)/shard_map/all_gather | solution.py:77
  49.0 0.1 reshape.136
  49.1 0.6 gather_fusion
  49.7 4.9 %slice_bitcast_fusion = (bf16[4,16,16,8,128]{4,3,2,1,0:T(8,128)(2,1)}, bf16[4,128,2048]{2,1,0:T(8,128)(2,1)}) fusion(bf16[4,128,4096]{2,1,0:T(8,128)(2,1)} %param.12), kind=kLoop, calls=%fused_computation.27 | loop fusion | bytes 8388608
  54.6 3.0 %copy.32 = bf16[4,128,2048]{1,2,0:T(8,128)(2,1)S(1)} copy(bf16[4,128,2048]{2,1,0:T(8,128)(2,1)} %get-tuple-element.38) | data formatting | bytes 4194304 | tf_op jit(solution)/shard_map/reshape | solution.py:39
  57.6 0.6 fusion.30
  58.2 0.1 fusion.21
  58.3 0.2 fusion.24
  58.5 2.2 fusion.15
  60.8 36.7 %all-gather.3 = bf16[32,4,16]{2,1,0:T(4,128)(2,1)S(1)} all-gather(bf16[1,4,16]{2,1,0:T(4,128)(2,1)S(1)} %bitcast.80), channel_id=1, replica_groups=mesh['req'=32] {'req'}, dimensions={0}, use_global_device_ids=true | all-gather | bytes 4224 | tf_op jit(solution)/shard_map/all_gather | solution.py:87
  97.5 38.0 %all-gather.2 = bf16[32,4,16]{2,1,0:T(4,128)(2,1)S(1)} all-gather(bf16[1,4,16]{2,1,0:T(4,128)(2,1)S(1)} %convert_bitcast_fusion.1), channel_id=1, replica_groups=mesh['req'=32] {'req'}, dimensions={0}, use_global_device_ids=true | all-gather | bytes 4224 | tf_op jit(solution)/shard_map/all_gather | solution.py:84
  135.5 0.6 gather_fusion.2
  136.0 0.6 gather_fusion.3
  136.6 0.1 broadcast_bitcast_fusion.2
  136.7 0.1 broadcast_bitcast_fusion
  136.8 38.1 %all-gather.1 = bf16[32,4,2048]{2,1,0:T(4,128)(2,1)S(1)} all-gather(bf16[1,4,2048]{2,1,0:T(4,128)(2,1)S(1)} %reshape.137), channel_id=1, replica_groups=mesh['req'=32] {'req'}, dimensions={0}, use_global_device_ids=true | all-gather | bytes 540672 | tf_op jit(solution)/shard_map/all_gather | solution.py:81
  174.8 0.1 reshape.143
  174.9 0.6 gather_fusion.1
  175.5 0.8 fusion.20
  176.3 0.0 copy-start
  176.3 50.8 %conditional.1 = (f32[512,2048]{1,0:T(8,128)}) conditional(s32[]{:T(128)} %bitcast.6, (bf16[4,2048]{1,0:T(4,128)(2,1)S(1)}, bf16[2048,2048]{1,0:T(8,128)(2,1)}) %tuple.13, (bf16[512,6144]{1,0:T(8,128)(2,1)}, bf16[2048,2048]{1,0:T(8,128)(2,1)}) %tuple.14), branch_computations={%region_3.4_spmd, %region_4.7_spmd} | conditional | flops 6493028352 | bytes 99778568 | solution.py:108
  176.5 0.1 iota_compare_fusion
  176.6 8.8 %copy.22 = bf16[512,6144]{0,1:T(8,128)(2,1)} copy(bf16[512,6144]{1,0:T(8,128)(2,1)} %get-tuple-element.27) | data formatting | bytes 12582912 | tf_op jit(solution)/shard_map
  185.4 4.6 %fusion.29 = (bf16[512,2048]{0,1:T(8,128)(2,1)S(1)}, bf16[512,2048]{0,1:T(8,128)(2,1)S(1)}, bf16[512,2048]{0,1:T(8,128)(2,1)}) fusion(bf16[512,6144]{0,1:T(8,128)(2,1)} %copy.22), kind=kLoop, calls=%fused_computation.58 | loop fusion | bytes 12582912 | tf_op jit(solution)/shard_map/cond/branch_1_fun/slice | solution.py:18
  190.0 7.5 %fusion = (f32[16,512]{1,0:T(8,128)S(1)}, f32[16,512,512]{1,2,0:T(8,128)}) fusion(pred[512,512]{0,1:T(8,128)(4,1)S(1)} %iota_compare_fusion, bf16[512,16,128]{0,2,1:T(8,128)(2,1)S(1)} %bitcast.72, bf16[512,16,128]{0,2,1:T(8,128)(2,1)S(1)} %bitcast.71), kind=kOutput, calls=%fused_computation.8 | convolution fusion | flops 1086316544 | bytes 21266432 | tf_op jit(solution)/shard_map/cond/branch_1_fun/qhd,khd->hqk/dot_general | solution.py:21
  197.5 9.1 %fusion.1 = f32[16,512]{1,0:T(8,128)S(1)} fusion(f32[16,512,512]{1,2,0:T(8,128)} %get-tuple-element.36, f32[16,512]{1,0:T(8,128)S(1)} %get-tuple-element.35, pred[512,512]{0,1:T(8,128)(4,1)S(1)} %iota_compare_fusion), kind=kLoop, calls=%fused_computation.9 | loop fusion | flops 16769024 | bytes 17104896 | tf_op jit(solution)/shard_map/cond/branch_1_fun/reduce_sum | solution.py:28
  206.7 10.9 %fusion.9 = bf16[512,16,128]{0,2,1:T(8,128)(2,1)S(1)} fusion(bf16[512,16,128]{0,2,1:T(8,128)(2,1)} %bitcast.73, f32[16,512,512]{1,2,0:T(8,128)} %get-tuple-element.36, f32[16,512]{1,0:T(8,128)S(1)} %get-tuple-element.35, pred[512,512]{0,1:T(8,128)(4,1)S(1)} %iota_compare_fusion, f32[512,16]{0,1:T(8,128)S(1)} %bitcast.78), kind=kOutput, calls=%fused_computation.17 | convolution fusion | flops 1092616192 | bytes 21299200 | tf_op jit(solution)/shard_map/cond/branch_1_fun/hqk,khd->qhd/dot_general | solution.py:29
  217.6 9.4 %fusion.10 = f32[512,2048]{1,0:T(8,128)} fusion(bf16[512,2048]{0,1:T(8,128)(2,1)S(1)} %bitcast.81, bf16[2048,2048]{1,0:T(8,128)(2,1)} %get-tuple-element.20), kind=kOutput, calls=%fused_computation.19 | convolution fusion | flops 4297064448 | bytes 14680064 | tf_op jit(solution)/shard_map/cond/branch_1_fun/dot_general | solution.py:98
  227.1 0.0 copy-done
  227.1 4.2 %add_convert_fusion = bf16[512,2048]{1,0:T(8,128)(2,1)} fusion(f32[512,2048]{1,0:T(8,128)} %get-tuple-element.43, bf16[512,2048]{1,0:T(8,128)(2,1)S(1)} %copy-done), kind=kLoop, calls=%fused_computation.23 | loop fusion | flops 3145728 | bytes 8388608 | tf_op jit(solution)/shard_map/convert_element_type | solution.py:110
  (9 shorter events, 0.1 us)
Async XLA Ops:
  176.3 50.8 %copy-start = (bf16[512,2048]{1,0:T(8,128)(2,1)S(1)}, bf16[512,2048]{1,0:T(8,128)(2,1)}, u32[]{:S(2)}) copy-start(bf16[512,2048]{1,0:T(8,128)(2,1)} %param.10) | copy-start | bytes 6291460
where the time goes:
time: 232 us; the launch traced here: 231 us
  blocking collectives  157 us (68%)
  matrix products  30.8 us (13%)
  local copies, waits for them, and re-layouts  24.7 us (11%)
  other arithmetic  17.4 us (7%)
    all_gather x1, blocking collectives, local(): every_query = lax.all_gather(request_rows[:, :D], 'req', axis=0, tiled=True)  44.6 us
    all_gather x1, blocking collectives, local(): lax.all_gather(part_out.astype(jnp.bfloat16), 'req', axis=0, tiled=True)  38.1 us
    all_gather x1, blocking collectives, local(): lax.all_gather(part_max.astype(jnp.bfloat16), 'req', axis=0, tiled=True)  38 us
    all_gather x1, blocking collectives, local(): lax.all_gather(part_total.astype(jnp.bfloat16), 'req', axis=0, tiled=True)  36.7 us
    dot_general x1, matrix products, prefill_attention(): jnp.einsum('hqk,khd->qhd', expon.astype(jnp.bfloat16), values_new, prefer...  10.9 us
    dot_general x1, matrix products, prefill_path(): jnp.dot(attended, out_weight, preferred_element_type=jnp.float32)  9.44 us
    reduce_sum x1, other arithmetic, prefill_attention(): totals = jnp.sum(expon, axis=-1)  9.15 us
    another operation x1, local copies, waits for them, and re-layouts  8.85 us

commit v1 on v0

--- a/solution.py
+++ b/solution.py
@@ -10,6 +10,18 @@
 TOK_DEV = 512
 RD = 4
 LMAX = 128
+
+
+def doubled_up(value, axis, dim):
+    ways, here, step = (lax.axis_size(axis), lax.axis_index(axis), value.shape[dim])
+    line, have = (value, 1)
+    while have < ways:
+        line = jnp.concatenate(
+            [line, lax.ppermute(line, axis, [(d, (d - have) % ways) for d in range(ways)])],
+            axis=dim,
+        )
+        have = 2 * have
+    return jnp.roll(line, here * step, axis=dim)
 
 
 def prefill_attention(block):
@@ -78,9 +90,7 @@
     held_queries = every_query[slot_owner]
     part_out, part_max, part_total = holder_partial(held_queries, cache, lengths)
     every_out, every_max, every_total = (
-        lax.all_gather(part_out.astype(jnp.bfloat16), "req", axis=0, tiled=True).astype(
-            part_out.dtype
-        ),
+        doubled_up(part_out.astype(jnp.bfloat16), "req", 0).astype(part_out.dtype),
         lax.all_gather(part_max.astype(jnp.bfloat16), "req", axis=0, tiled=True).astype(
             part_max.dtype
         ),

time: 232 us -> 220 us (0.948)
  blocking collectives: 157 us -> 123 us
  waiting for transfers between devices: 0 us -> 22 us
    all_gather x1 -> x0, blocking collectives: 38.1 us -> none  [local(): lax.all_gather(part_out.astype(jnp.bfloat16), 'req', axis=0, tiled=True)]
    ppermute x0 -> x5, waiting for transfers between devices: none -> 22 us  [doubled_up(): lax.ppermute(line, axis, [(d, (d - have) % ways) for d in range(ways)])]
    all_gather x1, blocking collectives: 38 us -> 41.7 us  [local(): lax.all_gather(part_max.astype(jnp.bfloat16), 'req', axis=0, tiled=True)]
    unnamed x8 -> x10, local copies, waits for them, and re-layouts: 5.91 us -> 5.89 us
  transfers between devices with their start and end apart: 0 -> 5, of which waited for: 0 -> 4; matrix products, arithmetic and copies ran while one was open for 0% -> 1% of each run, Pallas kernels for 0% -> 0%
where the time goes in v1:
time: 220 us; the launch traced here: 219 us
  blocking collectives  123 us (56%)
  matrix products  30.8 us (14%)
  local copies, waits for them, and re-layouts  25 us (11%)
  waiting for transfers between devices  22 us (10%)
  other arithmetic  17 us (8%)
    all_gather x1, blocking collectives, local(): every_query = lax.all_gather(request_rows[:, :D], 'req', axis=0, tiled=True)  44.6 us
    all_gather x1, blocking collectives, local(): lax.all_gather(part_max.astype(jnp.bfloat16), 'req', axis=0, tiled=True)  41.7 us
    all_gather x1, blocking collectives, local(): lax.all_gather(part_total.astype(jnp.bfloat16), 'req', axis=0, tiled=True)  36.6 us
    ppermute x5, waiting for transfers between devices, doubled_up(): lax.ppermute(line, axis, [(d, (d - have) % ways) for d in range(ways)])  22 us
    dot_general x1, matrix products, prefill_attention(): jnp.einsum('hqk,khd->qhd', expon.astype(jnp.bfloat16), values_new, prefer...  10.9 us
    dot_general x1, matrix products, prefill_path(): jnp.dot(attended, out_weight, preferred_element_type=jnp.float32)  9.45 us
    reduce_sum x1, other arithmetic, prefill_attention(): totals = jnp.sum(expon, axis=-1)  9.15 us
    another operation x1, local copies, waits for them, and re-layouts  8.83 us
  transfers between devices with their start and end apart: 5, of which 4 were waited for; matrix products, arithmetic and copies ran while one was open for 1% of the time, Pallas kernels for 0%

profile of v1, /device:TPU:0, one launch (start us, length us, event | category | flops | bytes accessed | tf_op | source)
XLA Modules:
  0.0 219.1 jit_solution(1134519120935969911)
XLA Ops:
  0.0 0.7 iota_compare_fusion.1
  0.7 0.7 compare_select_fusion.1
  1.4 0.8 slice_bitcast_fusion.1
  2.2 44.6 %all-gather = bf16[32,4,2048]{2,1,0:T(4,128)(2,1)S(1)} all-gather(bf16[1,4,2048]{2,1,0:T(4,128)(2,1)S(1)} %slice_bitcast_fusion.1), channel_id=1, replica_groups=mesh['req'=32] {'req'}, dimensions={0}, use_global_device_ids=true | all-gather | bytes 540672 | tf_op jit(solution)/shard_map/all_gather | solution.py:89
  46.8 0.1 reshape.136
  46.9 0.6 gather_fusion
  47.5 4.8 %slice_bitcast_fusion = (bf16[4,16,16,8,128]{4,3,2,1,0:T(8,128)(2,1)}, bf16[4,128,2048]{2,1,0:T(8,128)(2,1)}) fusion(bf16[4,128,4096]{2,1,0:T(8,128)(2,1)} %param.12), kind=kLoop, calls=%fused_computation.27 | loop fusion | bytes 8388608
  52.4 0.0 copy-start.1
  52.4 3.0 %copy.32 = bf16[4,128,2048]{1,2,0:T(8,128)(2,1)S(1)} copy(bf16[4,128,2048]{2,1,0:T(8,128)(2,1)} %get-tuple-element.38) | data formatting | bytes 4194304 | tf_op jit(solution)/shard_map/reshape | solution.py:51
  55.4 0.6 fusion.30
  56.1 0.1 fusion.21
  56.1 0.2 fusion.24
  56.3 2.2 %fusion.15 = f32[4,16,1,128]{3,2,1,0:T(1,128)S(1)} fusion(bf16[4,16,16,8,128]{4,3,2,1,0:T(8,128)(2,1)} %get-tuple-element.37, bf16[4,16,128,1]{2,1,0,3:T(8,128)(2,1)S(1)} %get-tuple-element.39), kind=kOutput, calls=%fused_computation.24 | convolution fusion | flops 2097152 | bytes 2146304 | tf_op jit(solution)/shard_map/rhl,rlhd->rhd/dot_general | solution.py:62
  58.6 0.1 collective-permute-start
  58.7 0.8 multiply_bitcast_fusion
  59.5 0.0 copy-done.1
  59.5 0.6 collective-permute-done
  60.1 0.1 collective-permute-start.1
  60.2 41.7 %all-gather.1 = bf16[32,4,16]{2,1,0:T(4,128)(2,1)S(1)} all-gather(bf16[1,4,16]{2,1,0:T(4,128)(2,1)S(1)} %convert_bitcast_fusion.2), channel_id=1, replica_groups=mesh['req'=32] {'req'}, dimensions={0}, use_global_device_ids=true | all-gather | bytes 4224 | tf_op jit(solution)/shard_map/all_gather | solution.py:94
  101.9 36.6 %all-gather.2 = bf16[32,4,16]{2,1,0:T(4,128)(2,1)S(1)} all-gather(bf16[1,4,16]{2,1,0:T(4,128)(2,1)S(1)} %bitcast.92), channel_id=1, replica_groups=mesh['req'=32] {'req'}, dimensions={0}, use_global_device_ids=true | all-gather | bytes 4224 | tf_op jit(solution)/shard_map/all_gather | solution.py:97
  138.6 0.6 gather_fusion.2
  139.1 0.6 gather_fusion.3
  139.7 0.0 collective-permute-done.1
  139.7 0.1 collective-permute-start.2
  139.8 0.1 bitcast_reduce_fusion
  139.9 4.2 %collective-permute-done.2 = bf16[16,2048]{1,0:T(8,128)(2,1)S(1)} collective-permute-done((bf16[16,2048]{1,0:T(8,128)(2,1)S(1)}, bf16[16,2048]{1,0:T(8,128)(2,1)S(1)}, u32[]{:S(2)}, u32[]{:S(2)}) %collective-permute-start.2) | collective-permute-done | bytes 65568 | tf_op jit(solution)/shard_map/ppermute | solution.py:20
  144.1 0.1 collective-permute-start.3
  144.2 4.9 %collective-permute-done.3 = bf16[32,2048]{1,0:T(8,128)(2,1)S(1)} collective-permute-done((bf16[32,2048]{1,0:T(8,128)(2,1)S(1)}, bf16[32,2048]{1,0:T(8,128)(2,1)S(1)}, u32[]{:S(2)}, u32[]{:S(2)}) %collective-permute-start.3) | collective-permute-done | bytes 131104 | tf_op jit(solution)/shard_map/ppermute | solution.py:20
  149.2 0.1 collective-permute-start.4
  149.3 0.1 broadcast_bitcast_fusion.2
  150.0 0.1 broadcast_bitcast_fusion
  150.1 12.2 %collective-permute-done.4 = bf16[64,2048]{1,0:T(8,128)(2,1)S(1)} collective-permute-done((bf16[64,2048]{1,0:T(8,128)(2,1)S(1)}, bf16[64,2048]{1,0:T(8,128)(2,1)S(1)}, u32[]{:S(2)}, u32[]{:S(2)}) %collective-permute-start.4) | collective-permute-done | bytes 262176 | tf_op jit(solution)/shard_map/ppermute | solution.py:20
  162.3 0.3 concatenate.29
  162.6 0.1 dynamic-slice_convert_fusion
  162.7 0.6 gather_fusion.1
  163.3 0.8 fusion.20
  164.1 0.0 copy-start
  164.1 50.8 %conditional.1 = (f32[512,2048]{1,0:T(8,128)}) conditional(s32[]{:T(128)} %bitcast.6, (bf16[4,2048]{1,0:T(4,128)(2,1)S(1)}, bf16[2048,2048]{1,0:T(8,128)(2,1)}) %tuple.13, (bf16[512,6144]{1,0:T(8,128)(2,1)}, bf16[2048,2048]{1,0:T(8,128)(2,1)}) %tuple.14), branch_computations={%region_3.4_spmd, %region_4.7_spmd} | conditional | flops 6493028352 | bytes 99778568 | solution.py:118
  164.3 0.1 iota_compare_fusion
  164.4 8.8 %copy.22 = bf16[512,6144]{0,1:T(8,128)(2,1)} copy(bf16[512,6144]{1,0:T(8,128)(2,1)} %get-tuple-element.27) | data formatting | bytes 12582912 | tf_op jit(solution)/shard_map
  173.2 4.6 %fusion.29 = (bf16[512,2048]{0,1:T(8,128)(2,1)S(1)}, bf16[512,2048]{0,1:T(8,128)(2,1)S(1)}, bf16[512,2048]{0,1:T(8,128)(2,1)}) fusion(bf16[512,6144]{0,1:T(8,128)(2,1)} %copy.22), kind=kLoop, calls=%fused_computation.64 | loop fusion | bytes 12582912 | tf_op jit(solution)/shard_map/cond/branch_1_fun/slice | solution.py:30
  177.8 7.5 %fusion = (f32[16,512]{1,0:T(8,128)S(1)}, f32[16,512,512]{1,2,0:T(8,128)}) fusion(pred[512,512]{0,1:T(8,128)(4,1)S(1)} %iota_compare_fusion, bf16[512,16,128]{0,2,1:T(8,128)(2,1)S(1)} %bitcast.77, bf16[512,16,128]{0,2,1:T(8,128)(2,1)S(1)} %bitcast.76), kind=kOutput, calls=%fused_computation.8 | convolution fusion | flops 1086316544 | bytes 21266432 | tf_op jit(solution)/shard_map/cond/branch_1_fun/qhd,khd->hqk/dot_general | solution.py:33
  185.4 9.1 %fusion.1 = f32[16,512]{1,0:T(8,128)S(1)} fusion(f32[16,512,512]{1,2,0:T(8,128)} %get-tuple-element.36, f32[16,512]{1,0:T(8,128)S(1)} %get-tuple-element.35, pred[512,512]{0,1:T(8,128)(4,1)S(1)} %iota_compare_fusion), kind=kLoop, calls=%fused_computation.9 | loop fusion | flops 16769024 | bytes 17104896 | tf_op jit(solution)/shard_map/cond/branch_1_fun/reduce_sum | solution.py:40
  194.5 10.9 %fusion.9 = bf16[512,16,128]{0,2,1:T(8,128)(2,1)S(1)} fusion(bf16[512,16,128]{0,2,1:T(8,128)(2,1)} %bitcast.78, f32[16,512,512]{1,2,0:T(8,128)} %get-tuple-element.36, f32[16,512]{1,0:T(8,128)S(1)} %get-tuple-element.35, pred[512,512]{0,1:T(8,128)(4,1)S(1)} %iota_compare_fusion, f32[512,16]{0,1:T(8,128)S(1)} %bitcast.90), kind=kOutput, calls=%fused_computation.17 | convolution fusion | flops 1092616192 | bytes 21299200 | tf_op jit(solution)/shard_map/cond/branch_1_fun/hqk,khd->qhd/dot_general | solution.py:41
  205.4 9.4 %fusion.10 = f32[512,2048]{1,0:T(8,128)} fusion(bf16[512,2048]{0,1:T(8,128)(2,1)S(1)} %bitcast.93, bf16[2048,2048]{1,0:T(8,128)(2,1)} %get-tuple-element.20), kind=kOutput, calls=%fused_computation.19 | convolution fusion | flops 4297064448 | bytes 14680064 | tf_op jit(solution)/shard_map/cond/branch_1_fun/dot_general | solution.py:108
  214.9 0.0 copy-done
  214.9 4.2 %add_convert_fusion = bf16[512,2048]{1,0:T(8,128)(2,1)} fusion(f32[512,2048]{1,0:T(8,128)} %get-tuple-element.43, bf16[512,2048]{1,0:T(8,128)(2,1)S(1)} %copy-done), kind=kLoop, calls=%fused_computation.23 | loop fusion | flops 3145728 | bytes 8388608 | tf_op jit(solution)/shard_map/convert_element_type | solution.py:120
  (14 shorter events, 0.2 us)
Async XLA Ops:
  52.4 7.1 %copy-start.1 = (s32[4]{0:T(128)S(1)}, s32[4]{0:T(128)}, u32[]{:S(2)}) copy-start(s32[4]{0:T(128)} %param.15) | copy-start | bytes 52
  58.6 1.5 collective-permute-start
  60.1 79.6 %collective-permute-start.1 = (bf16[8,2048]{1,0:T(8,128)(2,1)S(1)}, bf16[8,2048]{1,0:T(8,128)(2,1)S(1)}, u32[]{:S(2)}, u32[]{:S(2)}) collective-permute-start(bf16[8,2048]{1,0:T(8,128)(2,1)S(1)} %pad_maximum_fusion.2), channel_id=1, source_target_pairs={{0,30},{1,31},{2,0},{3,1},{4,2},{5,3},{6,4},{7,5},{8,6},{9,7},{10,... | collective-permute-start | bytes 98312 | tf_op jit(solution)/shard_map/ppermute | solution.py:20
  139.7 4.4 %collective-permute-start.2 = (bf16[16,2048]{1,0:T(8,128)(2,1)S(1)}, bf16[16,2048]{1,0:T(8,128)(2,1)S(1)}, u32[]{:S(2)}, u32[]{:S(2)}) collective-permute-start(bf16[16,2048]{1,0:T(8,128)(2,1)S(1)} %pad_maximum_fusion.1), channel_id=1, source_target_pairs={{0,28},{1,29},{2,30},{3,31},{4,0},{5,1},{6,2},{7,3},{8,4},{9,5},{1... | collective-permute-start | bytes 196616 | tf_op jit(solution)/shard_map/ppermute | solution.py:20
  144.1 5.0 %collective-permute-start.3 = (bf16[32,2048]{1,0:T(8,128)(2,1)S(1)}, bf16[32,2048]{1,0:T(8,128)(2,1)S(1)}, u32[]{:S(2)}, u32[]{:S(2)}) collective-permute-start(bf16[32,2048]{1,0:T(8,128)(2,1)S(1)} %pad_maximum_fusion), channel_id=1, source_target_pairs={{0,24},{1,25},{2,26},{3,27},{4,28},{5,29},{6,30},{7,31},{8,0},{9,1... | collective-permute-start | bytes 393224 | tf_op jit(solution)/shard_map/ppermute | solution.py:20
  149.2 13.1 %collective-permute-start.4 = (bf16[64,2048]{1,0:T(8,128)(2,1)S(1)}, bf16[64,2048]{1,0:T(8,128)(2,1)S(1)}, u32[]{:S(2)}, u32[]{:S(2)}) collective-permute-start(bf16[64,2048]{1,0:T(8,128)(2,1)S(1)} %concatenate.28), channel_id=1, source_target_pairs={{0,16},{1,17},{2,18},{3,19},{4,20},{5,21},{6,22},{7,23},{8,24},{9,... | collective-permute-start | bytes 786440 | tf_op jit(solution)/shard_map/ppermute | solution.py:20
  164.1 50.8 %copy-start = (bf16[512,2048]{1,0:T(8,128)(2,1)S(1)}, bf16[512,2048]{1,0:T(8,128)(2,1)}, u32[]{:S(2)}) copy-start(bf16[512,2048]{1,0:T(8,128)(2,1)} %param.10) | copy-start | bytes 6291460
